TPU v7x, 256 devices: a whole 4x4x8 slice. The times are simulated.
256 devices in a mesh: row: 16 (over z, core), col: 16 (over x, y).
Axes of the slice: x: 4, y: 4, z: 8, core: 2. Of those that a mesh axis runs over, the one named last changes fastest.
Arguments:
- tiles: float32 [16, 16, 16, 128, 128], P('row', 'col'), may hold values from -1 to 1
- tile_rows: int32 [16, 16, 16], P('row', 'col'), may hold values from 0 to 63, as said below
- tile_cols: int32 [16, 16, 16], P('row', 'col'), may hold values from 0 to 63
- tile_counts: int32 [16, 16], P('row', 'col'), may hold values from 2 to 16, as said below
- objective: float32 [131072], P('col'), may hold values from -6 to 6
- upper: float32 [131072], P('col'), may hold values from 0.2 to 2
- bound_codes: int32 [131072], P('col'), may hold values from 0 to 2
- rhs: float32 [131072], P('row'), may hold values from -6 to 6
- row_codes: int32 [131072], P('row'), may hold values from 0 to 1
Outputs:
- primal: float32 [131072], P('col')
- dual: float32 [131072], P('row')
Inputs may be any that keep to these rules, and one draw needn't show every extreme that they name: `tile_rows`: one device's live slots hold distinct (tile row, tile column) pairs. `tile_counts`: slots at or past a device's count are not part of K; some device has all 16 slots live.
All inputs are finite; a program needn't handle non-finite values. Where the computation divides by a largest or mean magnitude, that divisor is 1e-20 or more.
Results may differ from a plain program's by a relative error of at most 0.00018.
Values sent between devices are 32-bit elements; how exact they have to be, the bound alone decides.
A program may use at most 64 MiB of HBM per device.

v0:
```python
import jax
import jax.numpy as jnp
from jax import lax
from jax.sharding import PartitionSpec as P

TILE_BLOCK = 16
TILE_ROWS = 64
TILE_COLS = 64
OUTER = 2
INNER = 4


def project_primal(values, bound_codes, upper):
    values = jnp.where(bound_codes >= 1, jnp.maximum(values, 0.0), values)
    return jnp.where(bound_codes == 2, jnp.minimum(values, upper), values)


def project_dual(values, row_codes):
    return jnp.where(row_codes == 1, jnp.maximum(values, 0.0), values)


def step_update(step_size, weight, inter_term, primal_sq, dual_sq, counter):
    shrink = 1.0 - (counter + 1) ** (-0.3)
    growth = 1.0 + (counter + 1) ** (-0.6)
    numer = shrink * (weight * primal_sq + dual_sq / weight + 1e-06)
    return numer / jnp.maximum(2.0 * jnp.abs(inter_term), numer / (growth * step_size))


def tile_products(tile_data, row_slots, col_slots, live_count, vector, direction):
    highest = lax.Precision.HIGHEST
    width = tile_data.shape[-1]
    groups = (live_count + TILE_BLOCK - 1) // TILE_BLOCK
    if direction == "forward":
        shaped = vector.reshape(TILE_COLS, width)
        out_rows = TILE_ROWS
    else:
        shaped = vector.reshape(TILE_ROWS, width)
        out_rows = TILE_COLS

    def visit(group, total):
        first_slot = group * TILE_BLOCK
        alive = (first_slot + jnp.arange(TILE_BLOCK, dtype=jnp.int32) < live_count).astype(
            jnp.float32
        )
        row_hot = (row_slots[:, None] == jnp.arange(TILE_ROWS, dtype=jnp.int32)[None, :]).astype(
            jnp.float32
        )
        col_hot = (col_slots[:, None] == jnp.arange(TILE_COLS, dtype=jnp.int32)[None, :]).astype(
            jnp.float32
        )
        if direction == "forward":
            pieces = jnp.dot(col_hot, shaped, precision=highest)
            images = jnp.einsum("tij,tj->ti", tile_data, pieces, precision=highest)
            return total + jnp.einsum(
                "tk,ti->ki", row_hot * alive[:, None], images, precision=highest
            )
        else:
            pieces = jnp.dot(row_hot, shaped, precision=highest)
            images = jnp.einsum("tij,ti->tj", tile_data, pieces, precision=highest)
            return total + jnp.einsum(
                "tk,tj->kj", col_hot * alive[:, None], images, precision=highest
            )

    total = lax.fori_loop(0, groups, visit, jnp.zeros((out_rows, width), jnp.float32))
    return total.reshape(-1)


def per_device(
    tiles, tile_rows, tile_cols, tile_counts, objective, upper, bound_codes, rhs, row_codes
):
    tile_data = tiles[0, 0]
    row_slots = tile_rows[0, 0]
    col_slots = tile_cols[0, 0]
    live_count = tile_counts[0, 0]
    row_place = lax.axis_index("row")
    col_place = lax.axis_index("col")
    primal_mask = (row_place == 0).astype(jnp.float32)
    dual_mask = (col_place == 0).astype(jnp.float32)

    def forward(vector):
        partial_rows = tile_products(tile_data, row_slots, col_slots, live_count, vector, "forward")
        return lax.psum(partial_rows, "col")

    def backward(vector):
        partial_cols = tile_products(
            tile_data, row_slots, col_slots, live_count, vector, "backward"
        )
        return lax.psum(partial_cols, "row")

    def pair_sums(primal_term, dual_term):
        return lax.psum((primal_term * primal_mask, dual_term * dual_mask), ("row", "col"))

    alive_slots = (jnp.arange(tile_data.shape[0], dtype=jnp.int32) < live_count).astype(jnp.float32)
    local_largest = jnp.max(jnp.abs(tile_data) * alive_slots[:, None, None])
    largest = lax.pmax(local_largest, ("row", "col"))
    step_size = 0.05 / (largest + 1e-06)
    object_sq, rhs_sq = pair_sums(jnp.sum(objective * objective), jnp.sum(rhs * rhs))
    weight = jnp.sqrt((object_sq + 1e-06) / (rhs_sq + 1e-06))
    primal = jnp.zeros_like(objective)
    dual_piece = jnp.zeros_like(rhs)
    row_image = jnp.zeros_like(rhs)
    col_image = jnp.zeros_like(objective)
    counter = 0
    for cycle_index in range(OUTER):
        start_primal = primal
        start_dual = dual_piece
        primal_total = jnp.zeros_like(objective)
        dual_total = jnp.zeros_like(rhs)
        weight_total = jnp.zeros((), jnp.float32)
        for step_index in range(INNER):
            counter += 1
            next_primal = project_primal(
                primal - step_size / weight * (objective - col_image), bound_codes, upper
            )
            next_row = forward(next_primal)
            next_dual = project_dual(
                dual_piece + step_size * weight * (rhs - (2.0 * next_row - row_image)), row_codes
            )
            next_col = backward(next_dual)
            primal_move = next_primal - primal
            dual_move = next_dual - dual_piece
            inter_term, primal_sq, dual_sq = lax.psum(
                (
                    jnp.sum(primal_move * (next_col - col_image)) * primal_mask,
                    jnp.sum(primal_move * primal_move) * primal_mask,
                    jnp.sum(dual_move * dual_move) * dual_mask,
                ),
                ("row", "col"),
            )
            primal_total = primal_total + step_size * next_primal
            dual_total = dual_total + step_size * next_dual
            weight_total = weight_total + step_size
            step_size = step_update(step_size, weight, inter_term, primal_sq, dual_sq, counter)
            primal, dual_piece, row_image, col_image = (next_primal, next_dual, next_row, next_col)
        primal = primal_total / weight_total
        dual_piece = dual_total / weight_total
        primal_shift = primal - start_primal
        dual_shift = dual_piece - start_dual
        primal_drift, dual_drift = pair_sums(
            jnp.sum(primal_shift * primal_shift), jnp.sum(dual_shift * dual_shift)
        )
        weight = jnp.sqrt(weight * jnp.sqrt(dual_drift + 1e-06) / jnp.sqrt(primal_drift + 1e-06))
        if cycle_index + 1 < OUTER:
            row_image = forward(primal)
            col_image = backward(dual_piece)
    return (primal, dual_piece)


def solution(mesh):
    placed = (
        P("row", "col", None, None, None),
        P("row", "col", None),
        P("row", "col", None),
        P("row", "col"),
        P("col"),
        P("col"),
        P("col"),
        P("row"),
        P("row"),
    )
    return jax.shard_map(
        per_device, mesh=mesh, in_specs=placed, out_specs=(P("col"), P("row")), check_vma=False
    )
```

profile of v0, /device:TPU:32, one launch (start us, length us, event | category | flops | bytes accessed | tf_op | source)
XLA Modules:
  0.0 1723.5 jit_solution(5136370811758483441)
XLA Ops:
  10.5 79.8 %all-reduce.7 = (f32[]{:T(128)}, f32[]{:T(128)}) all-reduce(f32[]{:T(128)S(6)} %mul.700, f32[]{:T(128)S(6)} %mul.702), channel_id=1, replica_groups=mesh['row'=16,'col'=16] {'row','col'}, use_global_device_ids=true, to_apply=%region_1.0 | all-reduce | flops 2 | bytes 16 | tf_op jit(solution)/shard_map/psum | solution.py:91
  91.7 2.2 fusion.120
  93.9 73.6 %pmax.7 = f32[]{:T(128)} all-reduce(f32[]{:T(128)} %fusion.120), channel_id=1, replica_groups=mesh['row'=16,'col'=16] {'row','col'}, use_global_device_ids=true, to_apply=%region_5.0 | all-reduce | flops 1 | bytes 8 | tf_op jit(solution)/shard_map/pmax | solution.py:95
  169.1 1.7 fusion.117
  172.5 70.9 %psum.297 = f32[8192]{0:T(1024)S(1)} all-reduce(f32[8192]{0:T(1024)S(1)} %bitcast.318), channel_id=1, replica_groups=mesh['row'=16,'col'=16] {'col'}, use_global_device_ids=true, to_apply=%region_10.11 | all-reduce | flops 8192 | bytes 65536 | tf_op jit(solution)/shard_map/psum | solution.py:82
  246.2 42.2 %psum.299 = f32[8192]{0:T(1024)S(1)} all-reduce(f32[8192]{0:T(1024)S(1)} %bitcast.319), channel_id=1, replica_groups=mesh['row'=16,'col'=16] {'row'}, use_global_device_ids=true, to_apply=%region_15.16 | all-reduce | flops 8192 | bytes 65536 | tf_op jit(solution)/shard_map/psum | solution.py:88
  291.1 74.6 %all-reduce.6 = (f32[]{:T(128)}, f32[]{:T(128)}, f32[]{:T(128)}) all-reduce(f32[]{:T(128)S(6)} %mul.708, f32[]{:T(128)S(6)} %mul.715, f32[]{:T(128)S(6)} %mul.717), channel_id=1, replica_groups=mesh['row'=16,'col'=16] {'row','col'}, use_global_device_ids=true, to_apply=%region_7.8 | all-reduce | flops 3 | bytes 24 | tf_op jit(solution)/shard_map/psum | solution.py:122
  370.6 71.0 %psum.302 = f32[8192]{0:T(1024)S(1)} all-reduce(f32[8192]{0:T(1024)S(1)} %bitcast.320), channel_id=1, replica_groups=mesh['row'=16,'col'=16] {'col'}, use_global_device_ids=true, to_apply=%region_22.23 | all-reduce | flops 8192 | bytes 65536 | tf_op jit(solution)/shard_map/psum | solution.py:82
  444.4 42.2 %psum.304 = f32[8192]{0:T(1024)S(1)} all-reduce(f32[8192]{0:T(1024)S(1)} %bitcast.321), channel_id=1, replica_groups=mesh['row'=16,'col'=16] {'row'}, use_global_device_ids=true, to_apply=%region_27.28 | all-reduce | flops 8192 | bytes 65536 | tf_op jit(solution)/shard_map/psum | solution.py:88
  489.3 74.6 %all-reduce.5 = (f32[]{:T(128)}, f32[]{:T(128)}, f32[]{:T(128)}) all-reduce(f32[]{:T(128)S(6)} %mul.722, f32[]{:T(128)S(6)} %mul.729, f32[]{:T(128)S(6)} %mul.731), channel_id=1, replica_groups=mesh['row'=16,'col'=16] {'row','col'}, use_global_device_ids=true, to_apply=%region_19.20 | all-reduce | flops 3 | bytes 24 | tf_op jit(solution)/shard_map/psum | solution.py:122
  566.1 1.7 fusion.109
  568.8 71.0 %psum.307 = f32[8192]{0:T(1024)S(1)} all-reduce(f32[8192]{0:T(1024)S(1)} %bitcast.322), channel_id=1, replica_groups=mesh['row'=16,'col'=16] {'col'}, use_global_device_ids=true, to_apply=%region_34.35 | all-reduce | flops 8192 | bytes 65536 | tf_op jit(solution)/shard_map/psum | solution.py:82
  642.6 42.2 %psum.309 = f32[8192]{0:T(1024)S(1)} all-reduce(f32[8192]{0:T(1024)S(1)} %bitcast.323), channel_id=1, replica_groups=mesh['row'=16,'col'=16] {'row'}, use_global_device_ids=true, to_apply=%region_39.40 | all-reduce | flops 8192 | bytes 65536 | tf_op jit(solution)/shard_map/psum | solution.py:88
  687.5 74.6 %all-reduce.4 = (f32[]{:T(128)}, f32[]{:T(128)}, f32[]{:T(128)}) all-reduce(f32[]{:T(128)S(6)} %mul.736, f32[]{:T(128)S(6)} %mul.743, f32[]{:T(128)S(6)} %mul.745), channel_id=1, replica_groups=mesh['row'=16,'col'=16] {'row','col'}, use_global_device_ids=true, to_apply=%region_31.32 | all-reduce | flops 3 | bytes 24 | tf_op jit(solution)/shard_map/psum | solution.py:122
  765.0 1.7 fusion.105
  767.7 71.0 %psum.312 = f32[8192]{0:T(1024)S(1)} all-reduce(f32[8192]{0:T(1024)S(1)} %bitcast.324), channel_id=1, replica_groups=mesh['row'=16,'col'=16] {'col'}, use_global_device_ids=true, to_apply=%region_46.47 | all-reduce | flops 8192 | bytes 65536 | tf_op jit(solution)/shard_map/psum | solution.py:82
  845.0 1.7 fusion.97
  850.3 88.5 %all-reduce.15.cloned.1.call-done = (f32[8192]{0:T(1024)}, f32[8192]{0:T(1024)}) async-done(((f32[8192]{0:T(1024)}, f32[8192]{0:T(1024)}), (f32[8192]{0:T(1024)}, f32[8192]{0:T(1024)})) %all-reduce.15.cloned.1.call-update) | async-done | bytes 65552 | tf_op jit(solution)/shard_map/psum | solution.py:88
  941.5 77.5 %all-reduce.3 = (f32[]{:T(128)}, f32[]{:T(128)}, f32[]{:T(128)}, f32[]{:T(128)}, f32[]{:T(128)}) all-reduce(f32[]{:T(128)S(6)} %mul.750, f32[]{:T(128)S(6)} %mul.757, f32[]{:T(128)S(6)} %mul.759, f32[]{:T(128)S(6)} %mul.775, f32[]{:T(128)S(6)} %mul.778), channel_id=1, replica_groups=mesh['row'=16,'col'=16] {'row','col'}, use_global_device_ids=true, to_apply=%region_43.44 | all-reduce | flops 5 | bytes 40 | tf_op jit(solution)/shard_map/psum | solution.py:122
  1022.6 1.7 fusion.99
  1026.0 88.5 %all-reduce.13.cloned.1.call-done = (f32[8192]{0:T(1024)}, f32[8192]{0:T(1024)}) async-done(((f32[8192]{0:T(1024)}, f32[8192]{0:T(1024)}), (f32[8192]{0:T(1024)}, f32[8192]{0:T(1024)})) %all-reduce.13.cloned.1.call-update) | async-done | bytes 65552 | tf_op jit(solution)/shard_map/psum | solution.py:82
  1118.1 43.5 %psum.323 = f32[8192]{0:T(1024)S(1)} all-reduce(f32[8192]{0:T(1024)S(1)} %bitcast.329), channel_id=1, replica_groups=mesh['row'=16,'col'=16] {'row'}, use_global_device_ids=true, to_apply=%region_73.74 | all-reduce | flops 8192 | bytes 65536 | tf_op jit(solution)/shard_map/psum | solution.py:88
  1164.2 77.8 %all-reduce.2 = (f32[]{:T(128)}, f32[]{:T(128)}, f32[]{:T(128)}) all-reduce(f32[]{:T(128)S(6)} %mul.783, f32[]{:T(128)S(6)} %mul.790, f32[]{:T(128)S(6)} %mul.792), channel_id=1, replica_groups=mesh['row'=16,'col'=16] {'row','col'}, use_global_device_ids=true, to_apply=%region_62.63 | all-reduce | flops 3 | bytes 24 | tf_op jit(solution)/shard_map/psum | solution.py:122
  1244.4 1.7 fusion.93
  1247.1 70.4 %psum.326 = f32[8192]{0:T(1024)S(1)} all-reduce(f32[8192]{0:T(1024)S(1)} %bitcast.330), channel_id=1, replica_groups=mesh['row'=16,'col'=16] {'col'}, use_global_device_ids=true, to_apply=%region_80.81 | all-reduce | flops 8192 | bytes 65536 | tf_op jit(solution)/shard_map/psum | solution.py:82
  1320.3 42.5 %psum.328 = f32[8192]{0:T(1024)S(1)} all-reduce(f32[8192]{0:T(1024)S(1)} %bitcast.331), channel_id=1, replica_groups=mesh['row'=16,'col'=16] {'row'}, use_global_device_ids=true, to_apply=%region_85.86 | all-reduce | flops 8192 | bytes 65536 | tf_op jit(solution)/shard_map/psum | solution.py:88
  1365.5 74.6 %all-reduce.1 = (f32[]{:T(128)}, f32[]{:T(128)}, f32[]{:T(128)}) all-reduce(f32[]{:T(128)S(6)} %mul.799, f32[]{:T(128)S(6)} %mul.806, f32[]{:T(128)S(6)} %mul.808), channel_id=1, replica_groups=mesh['row'=16,'col'=16] {'row','col'}, use_global_device_ids=true, to_apply=%region_77.78 | all-reduce | flops 3 | bytes 24 | tf_op jit(solution)/shard_map/psum | solution.py:122
  1445.2 71.0 %psum.331 = f32[8192]{0:T(1024)S(1)} all-reduce(f32[8192]{0:T(1024)S(1)} %bitcast.332), channel_id=1, replica_groups=mesh['row'=16,'col'=16] {'col'}, use_global_device_ids=true, to_apply=%region_92.93 | all-reduce | flops 8192 | bytes 65536 | tf_op jit(solution)/shard_map/psum | solution.py:82
  1518.9 43.1 %psum.333 = f32[8192]{0:T(1024)S(1)} all-reduce(f32[8192]{0:T(1024)S(1)} %bitcast.333), channel_id=1, replica_groups=mesh['row'=16,'col'=16] {'row'}, use_global_device_ids=true, to_apply=%region_97.98 | all-reduce | flops 8192 | bytes 65536 | tf_op jit(solution)/shard_map/psum | solution.py:88
  1564.7 74.6 %all-reduce = (f32[]{:T(128)}, f32[]{:T(128)}, f32[]{:T(128)}) all-reduce(f32[]{:T(128)S(6)} %mul.815, f32[]{:T(128)S(6)} %mul.822, f32[]{:T(128)S(6)} %mul.824), channel_id=1, replica_groups=mesh['row'=16,'col'=16] {'row','col'}, use_global_device_ids=true, to_apply=%region_89.90 | all-reduce | flops 3 | bytes 24 | tf_op jit(solution)/shard_map/psum | solution.py:122
  1642.3 1.7 fusion.85
  1645.0 71.0 %psum.335 = f32[8192]{0:T(1024)S(1)} all-reduce(f32[8192]{0:T(1024)S(1)} %bitcast.317), channel_id=1, replica_groups=mesh['row'=16,'col'=16] {'col'}, use_global_device_ids=true, to_apply=%region_102.103 | all-reduce | flops 8192 | bytes 65536 | tf_op jit(solution)/shard_map/psum | solution.py:82
  (154 shorter events, 65.4 us)
Async XLA Ops:
  7.2 0.8 copy-start.1
  7.2 1.4 copy-start.2
  7.2 161.9 %copy-start = (f32[1,1,16,128,128]{4,3,2,1,0:T(8,128)S(1)}, f32[1,1,16,128,128]{4,3,2,1,0:T(8,128)}, u32[]{:S(2)}) copy-start(f32[1,1,16,128,128]{4,3,2,1,0:T(8,128)} %param.43) | copy-start | bytes 3145732
  7.2 931.6 %all-reduce.15.cloned.1.call-start = ((), (), s32[]{:S(2)}) async-start(), calls=%async_computation.1 | async-start | bytes 131072 | tf_op jit(solution)/shard_map/psum | solution.py:88
  91.7 76.6 %copy-start.3 = (f32[8192]{0:T(1024)S(1)}, f32[8192]{0:T(1024)}, u32[]{:S(2)}) copy-start(f32[8192]{0:T(1024)} %param.48) | copy-start | bytes 98308
  91.7 76.6 %copy-start.11 = (s32[8192]{0:T(1024)S(1)}, s32[8192]{0:T(1024)}, u32[]{:S(2)}) copy-start(s32[8192]{0:T(1024)} %param.49) | copy-start | bytes 98308
  168.3 0.7 copy-start.12
  170.9 0.7 copy-start.13
  172.5 70.9 %copy-start.10 = (s32[8192]{0:T(1024)S(1)}, s32[8192]{0:T(1024)}, u32[]{:S(2)}) copy-start(s32[8192]{0:T(1024)} %param.51) | copy-start | bytes 98308
  841.6 0.6 copy-start.4
  844.1 0.6 copy-start.5
  844.8 269.7 %all-reduce.13.cloned.1.call-start = ((), (), s32[]{:S(2)}) async-start(), calls=%async_computation | async-start | bytes 131072 | tf_op jit(solution)/shard_map/psum | solution.py:82
  847.8 0.6 copy-start.6
  940.2 82.1 %copy-start.8 = (f32[8192]{0:T(1024)S(1)}, f32[8192]{0:T(1024)}, u32[]{:S(2)}) copy-start(f32[8192]{0:T(1024)} %get-tuple-element.1828) | copy-start | bytes 98308
  1025.3 0.6 copy-start.7
  1247.1 70.4 %copy-start.9 = (f32[8192]{0:T(1024)S(1)}, f32[8192]{0:T(1024)}, u32[]{:S(2)}) copy-start(f32[8192]{0:T(1024)} %get-tuple-element.1827) | copy-start | bytes 98308
Sparse Core Ops, SparseCore 0:
  844.9 93.8 all-reduce.14
  1026.1 88.3 all-reduce.12
where the time goes:
time: 1730 us; the launch traced here: 1720 us
  blocking collectives  1430 us (83%)
  waiting for transfers between devices  177 us (10%)
  between operations  49.5 us (3%)
  matrix products  31.9 us (2%)
  other arithmetic  28 us (2%)
    psum x7, blocking collectives, per_device(): lax.psum((jnp.sum(primal_move * (next_col - col_image)) * primal_mask, jn...  528 us
    psum x7, blocking collectives, forward(): return lax.psum(partial_rows, 'col')  496 us
    psum x6, blocking collectives, backward(): return lax.psum(partial_cols, 'row')  256 us
    psum x1, waiting for transfers between devices, backward(): return lax.psum(partial_cols, 'row')  88.5 us
    psum x1, waiting for transfers between devices, forward(): return lax.psum(partial_rows, 'col')  88.5 us
    psum x1, blocking collectives, pair_sums(): lax.psum((primal_term * primal_mask, dual_term * dual_mask), ('row', 'col'))  79.8 us
    pmax x1, blocking collectives, per_device(): largest = lax.pmax(local_largest, ('row', 'col'))  73.6 us
  transfers between devices with their start and end apart: 2, of which 2 were waited for; matrix products, arithmetic and copies ran while one was open for 0% of the time, Pallas kernels for 0%

commit v1 on v0

--- a/solution.py
+++ b/solution.py
@@ -1,3 +1,4 @@
+import functools
 import jax
 import jax.numpy as jnp
 from jax import lax
@@ -8,6 +9,15 @@
 TILE_COLS = 64
 OUTER = 2
 INNER = 4
+
+
+def clear_types(message, along_axis):
+    part_now = jax.lax.all_gather(message, along_axis)
+    all_values = jnp.sum(part_now, 0)
+    return all_values
+
+
+loads_part = functools.partial(clear_types, along_axis="row")
 
 
 def project_primal(values, bound_codes, upper):
@@ -85,7 +95,7 @@
         partial_cols = tile_products(
             tile_data, row_slots, col_slots, live_count, vector, "backward"
         )
-        return lax.psum(partial_cols, "row")
+        return loads_part(partial_cols)
 
     def pair_sums(primal_term, dual_term):
         return lax.psum((primal_term * primal_mask, dual_term * dual_mask), ("row", "col"))

time: 1730 us -> 1510 us (0.87)
  blocking collectives: 1430 us -> 1300 us
  waiting for transfers between devices: 177 us -> 88 us
    psum x6 -> x0, blocking collectives: 256 us -> none  [backward(): return lax.psum(partial_cols, 'row')]
    all_gather x0 -> x8, blocking collectives: none -> 126 us  [clear_types(): part_now = jax.lax.all_gather(message, along_axis)]
    psum x1 -> x0, waiting for transfers between devices: 88.5 us -> none  [backward(): return lax.psum(partial_cols, 'row')]
  transfers between devices with their start and end apart: 2 -> 1, of which waited for: 2 -> 1; matrix products, arithmetic and copies ran while one was open for 0% -> 0% of each run, Pallas kernels for 0% -> 0%
where the time goes in v1:
time: 1510 us
  blocking collectives  1300 us (86%)
  waiting for transfers between devices  88 us (6%)
  between operations  49.4 us (3%)
  matrix products  31.9 us (2%)
  other arithmetic  29.9 us (2%)
    psum x7, blocking collectives, per_device(): lax.psum((jnp.sum(primal_move * (next_col - col_image)) * primal_mask, jn...  529 us
    psum x7, blocking collectives, forward(): return lax.psum(partial_rows, 'col')  495 us
    all_gather x8, blocking collectives, clear_types(): part_now = jax.lax.all_gather(message, along_axis)  126 us
    psum x1, waiting for transfers between devices, forward(): return lax.psum(partial_rows, 'col')  88 us
    psum x1, blocking collectives, pair_sums(): lax.psum((primal_term * primal_mask, dual_term * dual_mask), ('row', 'col'))  79.8 us
    pmax x1, blocking collectives, per_device(): largest = lax.pmax(local_largest, ('row', 'col'))  73.6 us
  transfers between devices with their start and end apart: 1, of which 1 were waited for; matrix products, arithmetic and copies ran while one was open for 0% of the time, Pallas kernels for 0%

profile of v1, /device:TPU:32, one launch (start us, length us, event | category | flops | bytes accessed | tf_op | source)
XLA Modules:
  0.0 1505.8 jit_solution(9867328412182189689)
XLA Ops:
  10.5 79.8 %all-reduce.7 = (f32[]{:T(128)}, f32[]{:T(128)}) all-reduce(f32[]{:T(128)S(6)} %mul.700, f32[]{:T(128)S(6)} %mul.702), channel_id=1, replica_groups=mesh['row'=16,'col'=16] {'row','col'}, use_global_device_ids=true, to_apply=%region_1.0 | all-reduce | flops 2 | bytes 16 | tf_op jit(solution)/shard_map/psum | solution.py:101
  91.7 2.2 fusion.120
  93.9 73.6 %pmax.7 = f32[]{:T(128)} all-reduce(f32[]{:T(128)} %fusion.120), channel_id=1, replica_groups=mesh['row'=16,'col'=16] {'row','col'}, use_global_device_ids=true, to_apply=%region_5.0 | all-reduce | flops 1 | bytes 8 | tf_op jit(solution)/shard_map/pmax | solution.py:105
  169.1 1.7 fusion.117
  172.5 70.9 %psum.241 = f32[8192]{0:T(1024)S(1)} all-reduce(f32[8192]{0:T(1024)S(1)} %bitcast.326), channel_id=1, replica_groups=mesh['row'=16,'col'=16] {'col'}, use_global_device_ids=true, to_apply=%region_10.11 | all-reduce | flops 8192 | bytes 65536 | tf_op jit(solution)/shard_map/psum | solution.py:92
  246.2 15.5 %all-gather = f32[16,1,8192]{2,1,0:T(1,128)S(1)} all-gather(f32[1,1,8192]{2,1,0:T(1,128)S(1)} %bitcast.317), channel_id=1, replica_groups=mesh['row'=16,'col'=16] {'row'}, dimensions={0}, use_global_device_ids=true | all-gather | bytes 557056 | tf_op jit(solution)/shard_map/all_gather | solution.py:15
  264.8 75.5 %all-reduce.6 = (f32[]{:T(128)}, f32[]{:T(128)}, f32[]{:T(128)}) all-reduce(f32[]{:T(128)S(6)} %mul.708, f32[]{:T(128)S(6)} %mul.715, f32[]{:T(128)S(6)} %mul.717), channel_id=1, replica_groups=mesh['row'=16,'col'=16] {'row','col'}, use_global_device_ids=true, to_apply=%region_7.8 | all-reduce | flops 3 | bytes 24 | tf_op jit(solution)/shard_map/psum | solution.py:132
  342.5 1.7 fusion.113
  345.2 70.7 %psum.245 = f32[8192]{0:T(1024)S(1)} all-reduce(f32[8192]{0:T(1024)S(1)} %bitcast.327), channel_id=1, replica_groups=mesh['row'=16,'col'=16] {'col'}, use_global_device_ids=true, to_apply=%region_22.23 | all-reduce | flops 8192 | bytes 65536 | tf_op jit(solution)/shard_map/psum | solution.py:92
  418.7 15.5 %all-gather.1 = f32[16,1,8192]{2,1,0:T(1,128)S(1)} all-gather(f32[1,1,8192]{2,1,0:T(1,128)S(1)} %bitcast.318), channel_id=1, replica_groups=mesh['row'=16,'col'=16] {'row'}, dimensions={0}, use_global_device_ids=true | all-gather | bytes 557056 | tf_op jit(solution)/shard_map/all_gather | solution.py:15
  437.2 75.5 %all-reduce.5 = (f32[]{:T(128)}, f32[]{:T(128)}, f32[]{:T(128)}) all-reduce(f32[]{:T(128)S(6)} %mul.722, f32[]{:T(128)S(6)} %mul.729, f32[]{:T(128)S(6)} %mul.731), channel_id=1, replica_groups=mesh['row'=16,'col'=16] {'row','col'}, use_global_device_ids=true, to_apply=%region_19.20 | all-reduce | flops 3 | bytes 24 | tf_op jit(solution)/shard_map/psum | solution.py:132
  517.7 70.8 %psum.249 = f32[8192]{0:T(1024)S(1)} all-reduce(f32[8192]{0:T(1024)S(1)} %bitcast.328), channel_id=1, replica_groups=mesh['row'=16,'col'=16] {'col'}, use_global_device_ids=true, to_apply=%region_34.35 | all-reduce | flops 8192 | bytes 65536 | tf_op jit(solution)/shard_map/psum | solution.py:92
  591.3 15.5 %all-gather.2 = f32[16,1,8192]{2,1,0:T(1,128)S(1)} all-gather(f32[1,1,8192]{2,1,0:T(1,128)S(1)} %bitcast.319), channel_id=1, replica_groups=mesh['row'=16,'col'=16] {'row'}, dimensions={0}, use_global_device_ids=true | all-gather | bytes 557056 | tf_op jit(solution)/shard_map/all_gather | solution.py:15
  609.9 75.5 %all-reduce.4 = (f32[]{:T(128)}, f32[]{:T(128)}, f32[]{:T(128)}) all-reduce(f32[]{:T(128)S(6)} %mul.736, f32[]{:T(128)S(6)} %mul.743, f32[]{:T(128)S(6)} %mul.745), channel_id=1, replica_groups=mesh['row'=16,'col'=16] {'row','col'}, use_global_device_ids=true, to_apply=%region_31.32 | all-reduce | flops 3 | bytes 24 | tf_op jit(solution)/shard_map/psum | solution.py:132
  688.3 1.7 fusion.105
  691.0 70.7 %psum.253 = f32[8192]{0:T(1024)S(1)} all-reduce(f32[8192]{0:T(1024)S(1)} %bitcast.329), channel_id=1, replica_groups=mesh['row'=16,'col'=16] {'col'}, use_global_device_ids=true, to_apply=%region_46.47 | all-reduce | flops 8192 | bytes 65536 | tf_op jit(solution)/shard_map/psum | solution.py:92
  765.1 15.5 %all-gather.3 = f32[16,1,8192]{2,1,0:T(1,128)S(1)} all-gather(f32[1,1,8192]{2,1,0:T(1,128)S(1)} %bitcast.320), channel_id=1, replica_groups=mesh['row'=16,'col'=16] {'row'}, dimensions={0}, use_global_device_ids=true | all-gather | bytes 557056 | tf_op jit(solution)/shard_map/all_gather | solution.py:15
  784.7 75.6 %all-reduce.3 = (f32[]{:T(128)}, f32[]{:T(128)}, f32[]{:T(128)}, f32[]{:T(128)}, f32[]{:T(128)}) all-reduce(f32[]{:T(128)S(6)} %mul.750, f32[]{:T(128)S(6)} %mul.757, f32[]{:T(128)S(6)} %mul.759, f32[]{:T(128)S(6)} %mul.775, f32[]{:T(128)S(6)} %mul.778), channel_id=1, replica_groups=mesh['row'=16,'col'=16] {'row','col'}, use_global_device_ids=true, to_apply=%region_43.44 | all-reduce | flops 5 | bytes 40 | tf_op jit(solution)/shard_map/psum | solution.py:132
  865.9 15.5 %all-gather.4 = f32[16,1,8192]{2,1,0:T(1,128)S(1)} all-gather(f32[1,1,8192]{2,1,0:T(1,128)S(1)} %bitcast.321), channel_id=1, replica_groups=mesh['row'=16,'col'=16] {'row'}, dimensions={0}, use_global_device_ids=true | all-gather | bytes 557056 | tf_op jit(solution)/shard_map/all_gather | solution.py:15
  882.2 1.7 fusion.99
  888.6 88.0 %all-reduce.11.cloned.1.call-done = (f32[8192]{0:T(1024)}, f32[8192]{0:T(1024)}) async-done(((f32[8192]{0:T(1024)}, f32[8192]{0:T(1024)}), (f32[8192]{0:T(1024)}, f32[8192]{0:T(1024)})) %all-reduce.11.cloned.1.call-update) | async-done | bytes 65552 | tf_op jit(solution)/shard_map/psum | solution.py:92
  980.1 17.5 %all-gather.5 = f32[16,1,8192]{2,1,0:T(1,128)S(1)} all-gather(f32[1,1,8192]{2,1,0:T(1,128)S(1)} %bitcast.322), channel_id=1, replica_groups=mesh['row'=16,'col'=16] {'row'}, dimensions={0}, use_global_device_ids=true | all-gather | bytes 557056 | tf_op jit(solution)/shard_map/all_gather | solution.py:15
  1000.5 75.8 %all-reduce.2 = (f32[]{:T(128)}, f32[]{:T(128)}, f32[]{:T(128)}) all-reduce(f32[]{:T(128)S(6)} %mul.783, f32[]{:T(128)S(6)} %mul.790, f32[]{:T(128)S(6)} %mul.792), channel_id=1, replica_groups=mesh['row'=16,'col'=16] {'row','col'}, use_global_device_ids=true, to_apply=%region_62.63 | all-reduce | flops 3 | bytes 24 | tf_op jit(solution)/shard_map/psum | solution.py:132
  1081.4 70.9 %psum.264 = f32[8192]{0:T(1024)S(1)} all-reduce(f32[8192]{0:T(1024)S(1)} %bitcast.332), channel_id=1, replica_groups=mesh['row'=16,'col'=16] {'col'}, use_global_device_ids=true, to_apply=%region_80.81 | all-reduce | flops 8192 | bytes 65536 | tf_op jit(solution)/shard_map/psum | solution.py:92
  1155.0 15.5 %all-gather.6 = f32[16,1,8192]{2,1,0:T(1,128)S(1)} all-gather(f32[1,1,8192]{2,1,0:T(1,128)S(1)} %bitcast.323), channel_id=1, replica_groups=mesh['row'=16,'col'=16] {'row'}, dimensions={0}, use_global_device_ids=true | all-gather | bytes 557056 | tf_op jit(solution)/shard_map/all_gather | solution.py:15
  1173.6 75.5 %all-reduce.1 = (f32[]{:T(128)}, f32[]{:T(128)}, f32[]{:T(128)}) all-reduce(f32[]{:T(128)S(6)} %mul.799, f32[]{:T(128)S(6)} %mul.806, f32[]{:T(128)S(6)} %mul.808), channel_id=1, replica_groups=mesh['row'=16,'col'=16] {'row','col'}, use_global_device_ids=true, to_apply=%region_77.78 | all-reduce | flops 3 | bytes 24 | tf_op jit(solution)/shard_map/psum | solution.py:132
  1251.4 1.7 fusion.89
  1254.2 70.7 %psum.268 = f32[8192]{0:T(1024)S(1)} all-reduce(f32[8192]{0:T(1024)S(1)} %bitcast.333), channel_id=1, replica_groups=mesh['row'=16,'col'=16] {'col'}, use_global_device_ids=true, to_apply=%region_92.93 | all-reduce | flops 8192 | bytes 65536 | tf_op jit(solution)/shard_map/psum | solution.py:92
  1327.6 15.5 %all-gather.7 = f32[16,1,8192]{2,1,0:T(1,128)S(1)} all-gather(f32[1,1,8192]{2,1,0:T(1,128)S(1)} %bitcast.324), channel_id=1, replica_groups=mesh['row'=16,'col'=16] {'row'}, dimensions={0}, use_global_device_ids=true | all-gather | bytes 557056 | tf_op jit(solution)/shard_map/all_gather | solution.py:15
  1346.2 75.8 %all-reduce = (f32[]{:T(128)}, f32[]{:T(128)}, f32[]{:T(128)}) all-reduce(f32[]{:T(128)S(6)} %mul.815, f32[]{:T(128)S(6)} %mul.822, f32[]{:T(128)S(6)} %mul.824), channel_id=1, replica_groups=mesh['row'=16,'col'=16] {'row','col'}, use_global_device_ids=true, to_apply=%region_89.90 | all-reduce | flops 3 | bytes 24 | tf_op jit(solution)/shard_map/psum | solution.py:132
  1424.9 1.7 fusion.85
  1427.7 70.7 %psum.271 = f32[8192]{0:T(1024)S(1)} all-reduce(f32[8192]{0:T(1024)S(1)} %bitcast.325), channel_id=1, replica_groups=mesh['row'=16,'col'=16] {'col'}, use_global_device_ids=true, to_apply=%region_102.103 | all-reduce | flops 8192 | bytes 65536 | tf_op jit(solution)/shard_map/psum | solution.py:92
  (155 shorter events, 68.2 us)
Async XLA Ops:
  7.2 0.8 copy-start.1
  7.2 1.4 copy-start.2
  7.2 161.9 %copy-start = (f32[1,1,16,128,128]{4,3,2,1,0:T(8,128)S(1)}, f32[1,1,16,128,128]{4,3,2,1,0:T(8,128)}, u32[]{:S(2)}) copy-start(f32[1,1,16,128,128]{4,3,2,1,0:T(8,128)} %param.43) | copy-start | bytes 3145732
  7.2 969.4 %all-reduce.11.cloned.1.call-start = ((), (), s32[]{:S(2)}) async-start(), calls=%async_computation | async-start | bytes 131072 | tf_op jit(solution)/shard_map/psum | solution.py:92
  91.7 76.6 %copy-start.3 = (f32[8192]{0:T(1024)S(1)}, f32[8192]{0:T(1024)}, u32[]{:S(2)}) copy-start(f32[8192]{0:T(1024)} %param.48) | copy-start | bytes 98308
  91.7 76.6 %copy-start.8 = (s32[8192]{0:T(1024)S(1)}, s32[8192]{0:T(1024)}, u32[]{:S(2)}) copy-start(s32[8192]{0:T(1024)} %param.49) | copy-start | bytes 98308
  168.3 0.7 copy-start.9
  170.9 0.7 copy-start.10
  172.5 70.9 %copy-start.7 = (s32[8192]{0:T(1024)S(1)}, s32[8192]{0:T(1024)}, u32[]{:S(2)}) copy-start(s32[8192]{0:T(1024)} %param.51) | copy-start | bytes 98308
  884.9 1.7 copy-start.4
  887.9 0.6 copy-start.5
  1081.3 70.9 %copy-start.6 = (f32[8192]{0:T(1024)S(1)}, f32[8192]{0:T(1024)}, u32[]{:S(2)}) copy-start(f32[8192]{0:T(1024)} %get-tuple-element.1827) | copy-start | bytes 98308
Sparse Core Ops, SparseCore 0:
  888.7 87.8 all-reduce.10
